TPU v7x, 32 devices: a whole 2x2x4 slice. The times are simulated.
32 devices in a mesh: dp: 8 (over z, y), rep: 4 (over x, core).
Axes of the slice: x: 2, y: 2, z: 4, core: 2. Of those that a mesh axis runs over, the one named last changes fastest.
Arguments:
- cell_input: bfloat16 [16384, 1024], P(('dp', 'rep')), may hold values from -6 to 6
- cotangent: bfloat16 [16384, 1024], P(('dp', 'rep')), may hold values from -6 to 6
- segment_ids: int32 [32, 512], P(('dp', 'rep')), may hold values from 0 to 15, never falling along the last dimension, each value on 1 to 128 neighbouring positions
- lengths: int32 [32], P(('dp', 'rep')), may hold values from 256 to 512
- w_qkv: bfloat16 [1024, 3072], P('dp'), may hold values from -0.1875 to 0.1875
- query_bias: bfloat16 [1024], P('dp'), may hold values from -1.75 to 1.75
- value_bias: bfloat16 [1024], P('dp'), may hold values from -1.75 to 1.75
- w_out: bfloat16 [1024, 1024], P('dp'), may hold values from -1 to 1
- out_bias: bfloat16 [1024], P('dp'), may hold values from -1.75 to 1.75
- w_up: bfloat16 [1024, 4096], P('dp'), may hold values from -0.1875 to 0.1875
- up_bias: bfloat16 [4096], P('dp'), may hold values from -1.75 to 1.75
- w_down: bfloat16 [4096, 1024], P('dp'), may hold values from -0.09375 to 0.09375
- down_bias: bfloat16 [1024], P('dp'), may hold values from -1.75 to 1.75
- norm1_gain: bfloat16 [1024], P('dp'), may hold values from 0.5 to 1.5
- norm1_bias: bfloat16 [1024], P('dp'), may hold values from -1.75 to 1.75
- norm2_gain: bfloat16 [1024], P('dp'), may hold values from 0.5 to 1.5
- norm2_bias: bfloat16 [1024], P('dp'), may hold values from -1.75 to 1.75
Outputs:
- block_out: bfloat16 [16384, 1024], P(('dp', 'rep'))
- input_grad: bfloat16 [16384, 1024], P(('dp', 'rep'))
- grad_qkv: float32 [1024, 3072], P('dp')
- grad_query_bias: float32 [1024], P('dp')
- grad_value_bias: float32 [1024], P('dp')
- grad_out: float32 [1024, 1024], P('dp')
- grad_out_bias: float32 [1024], P('dp')
- grad_up: float32 [1024, 4096], P('dp')
- grad_up_bias: float32 [4096], P('dp')
- grad_down: float32 [4096, 1024], P('dp')
- grad_down_bias: float32 [1024], P('dp')
- grad_norm1_gain: float32 [1024], P('dp')
- grad_norm1_bias: float32 [1024], P('dp')
- grad_norm2_gain: float32 [1024], P('dp')
- grad_norm2_bias: float32 [1024], P('dp')
Inputs may be any that keep to these rules, and one draw needn't show every extreme that they name: `segment_ids`: in each sequence the ids never fall; each of the 16 slides holds 1 to 128 cells, and one holds exactly 128. `lengths`: rows of a sequence at or past its length are padding.
All inputs are finite; a program needn't handle non-finite values.
Results may differ from a plain program's by a relative error of at most 0.015.
Values may be sent and summed in bfloat16 or wider, within the bound.
No kernel may reach another device: no remote copies, remote signals or barrier semaphores. Data moves between devices by JAX's collectives and lax.ppermute only.
A program may use at most 192 MiB of HBM per device.

v0:
```python
import math

import jax
import jax.numpy as jnp
from jax import lax
from jax.sharding import PartitionSpec as P

HEAD_DIM = 64


def normalize(values_in):
    row_mean = jnp.mean(values_in, axis=-1, keepdims=True)
    centred = values_in - row_mean
    inv_std = lax.rsqrt(jnp.mean(centred * centred, axis=-1, keepdims=True) + 1e-05)
    return (centred * inv_std, inv_std)


def norm_back(incoming, normed, inv_std, gain_vec):
    scaled = incoming * gain_vec
    return inv_std * (
        scaled
        - jnp.mean(scaled, axis=-1, keepdims=True)
        - normed * jnp.mean(scaled * normed, axis=-1, keepdims=True)
    )


def positions(length, model_width):
    places = jnp.arange(length, dtype=jnp.float32)[:, None]
    frequency = jnp.exp(
        jnp.arange(model_width // 2, dtype=jnp.float32) * (-2.0 * math.log(10000.0) / model_width)
    )
    angles = places * frequency[None, :]
    return jnp.stack([jnp.sin(angles), jnp.cos(angles)], axis=-1).reshape(length, model_width)


def gelu_slope(values_in):
    normal_cdf = 0.5 * (1.0 + lax.erf(values_in * (1.0 / math.sqrt(2.0))))
    return normal_cdf + values_in * jnp.exp(-0.5 * values_in * values_in) * (
        1.0 / math.sqrt(2.0 * math.pi)
    )


def block_mask(begin_row, block_rows, seg_row, live_cells):
    places = jnp.arange(seg_row.shape[0], dtype=jnp.int32)
    rows_at = begin_row + jnp.arange(block_rows, dtype=jnp.int32)
    return (seg_row[:, None] == seg_row[None, :]) & live_cells[:, None] & live_cells[None, :] | (
        rows_at[:, None] == places[None, :]
    )


def masked_scores(block_q, key_vecs, begin_row, block_rows, seg_row, live_cells):
    score_scale = 1.0 / math.sqrt(HEAD_DIM)
    scores = (
        jnp.einsum("qhd,khd->hqk", block_q, key_vecs, preferred_element_type=jnp.float32)
        * score_scale
    )
    return jnp.where(block_mask(begin_row, block_rows, seg_row, live_cells)[None], scores, -1e30)


def attention_forward(queries, key_vecs, values, seg_row, live_cells, block_rows):
    begin_rows = jnp.arange(queries.shape[0] // block_rows, dtype=jnp.int32) * block_rows

    def query_block(begin_row):
        scores = masked_scores(queries, key_vecs, begin_row, block_rows, seg_row, live_cells)
        row_max = jnp.max(scores, axis=-1, keepdims=True)
        exp_scores = jnp.exp(scores - row_max)
        row_total = jnp.sum(exp_scores, axis=-1, keepdims=True)
        weights = (exp_scores / row_total).astype(jnp.bfloat16)
        attended = jnp.einsum("hqk,khd->qhd", weights, values, preferred_element_type=jnp.float32)
        return (attended.astype(jnp.bfloat16), (row_max + jnp.log(row_total))[..., 0])

    attended, log_totals = lax.map(query_block, begin_rows)
    return (attended.reshape(queries.shape), log_totals)


def attention_backward(
    queries, key_vecs, values, attended_grad, log_totals, seg_row, live_cells, block_rows
):
    score_scale = 1.0 / math.sqrt(HEAD_DIM)
    begin_rows = jnp.arange(queries.shape[0] // block_rows, dtype=jnp.int32) * block_rows

    def query_block(running, inputs):
        begin_row, block_log = inputs
        key_total, value_total = running
        scores = masked_scores(queries, key_vecs, begin_row, block_rows, seg_row, live_cells)
        weights_f = jnp.exp(scores - block_log[..., None])
        value_total = value_total + jnp.einsum(
            "hqk,qhd->khd",
            weights_f.astype(jnp.bfloat16),
            attended_grad,
            preferred_element_type=jnp.float32,
        )
        prob_grad = jnp.einsum(
            "qhd,khd->hqk", attended_grad, values, preferred_element_type=jnp.float32
        )
        dscore = (
            weights_f * (prob_grad - jnp.sum(prob_grad * weights_f, axis=-1, keepdims=True))
        ).astype(jnp.bfloat16)
        block_dq = (
            jnp.einsum("hqk,khd->qhd", dscore, key_vecs, preferred_element_type=jnp.float32)
            * score_scale
        ).astype(jnp.bfloat16)
        key_total = (
            key_total
            + jnp.einsum("hqk,qhd->khd", dscore, queries, preferred_element_type=jnp.float32)
            * score_scale
        )
        return ((key_total, value_total), block_dq)

    zero_acc = jnp.zeros(queries.shape, jnp.float32)
    (key_total, value_total), query_grad = lax.scan(
        query_block, (zero_acc, zero_acc), (begin_rows, log_totals)
    )
    return (
        query_grad.reshape(queries.shape),
        key_total.astype(jnp.bfloat16),
        value_total.astype(jnp.bfloat16),
    )


def forward_pass(gathered, cell_input, pos_table, seg_row, live_cells, block_rows):
    (
        w_qkv,
        query_bias,
        value_bias,
        w_out,
        out_bias,
        w_up,
        up_bias,
        w_down,
        down_bias,
        norm1_gain,
        norm1_bias,
        norm2_gain,
        norm2_bias,
    ) = gathered
    length, model_width = cell_input.shape
    head_count = model_width // HEAD_DIM
    cells_f = cell_input.astype(jnp.float32)
    normed_one, inv_one = normalize(cells_f)
    normed_in = (
        normed_one * norm1_gain.astype(jnp.float32) + norm1_bias.astype(jnp.float32) + pos_table
    ).astype(jnp.bfloat16)
    projected = jnp.dot(normed_in, w_qkv, preferred_element_type=jnp.float32)
    queries = (
        (projected[:, :model_width] + query_bias.astype(jnp.float32))
        .astype(jnp.bfloat16)
        .reshape(length, head_count, HEAD_DIM)
    )
    key_vecs = (
        projected[:, model_width : 2 * model_width]
        .astype(jnp.bfloat16)
        .reshape(length, head_count, HEAD_DIM)
    )
    values = (
        (projected[:, 2 * model_width :] + value_bias.astype(jnp.float32))
        .astype(jnp.bfloat16)
        .reshape(length, head_count, HEAD_DIM)
    )
    attended, log_totals = attention_forward(
        queries, key_vecs, values, seg_row, live_cells, block_rows
    )
    attended = attended.reshape(length, model_width)
    middle = (
        cells_f
        + jnp.dot(attended, w_out, preferred_element_type=jnp.float32)
        + out_bias.astype(jnp.float32)
    )
    normed_two, inv_two = normalize(middle)
    hidden_in = (
        normed_two * norm2_gain.astype(jnp.float32) + norm2_bias.astype(jnp.float32)
    ).astype(jnp.bfloat16)
    pre_act = jnp.dot(hidden_in, w_up, preferred_element_type=jnp.float32) + up_bias.astype(
        jnp.float32
    )
    hidden = jax.nn.gelu(pre_act, approximate=False).astype(jnp.bfloat16)
    result = (
        middle
        + jnp.dot(hidden, w_down, preferred_element_type=jnp.float32)
        + down_bias.astype(jnp.float32)
    )
    kept = (
        normed_in,
        normed_one,
        inv_one,
        queries,
        key_vecs,
        values,
        attended,
        log_totals,
        normed_two,
        inv_two,
        hidden_in,
        pre_act,
        hidden,
    )
    return (result.astype(jnp.bfloat16), kept)


def backward_pass(gathered, kept, cotangent, seg_row, live_cells, block_rows):
    (
        w_qkv,
        query_bias,
        value_bias,
        w_out,
        out_bias,
        w_up,
        up_bias,
        w_down,
        down_bias,
        norm1_gain,
        norm1_bias,
        norm2_gain,
        norm2_bias,
    ) = gathered
    (
        normed_in,
        normed_one,
        inv_one,
        queries,
        key_vecs,
        values,
        attended,
        log_totals,
        normed_two,
        inv_two,
        hidden_in,
        pre_act,
        hidden,
    ) = kept
    length = attended.shape[0]
    upstream = cotangent.astype(jnp.float32)
    grad_down = jnp.einsum("tf,td->fd", hidden, cotangent, preferred_element_type=jnp.float32)
    grad_down_bias = jnp.sum(upstream, axis=0)
    hidden_grad = jnp.einsum("td,fd->tf", cotangent, w_down, preferred_element_type=jnp.float32)
    pre_grad = (hidden_grad * gelu_slope(pre_act)).astype(jnp.bfloat16)
    grad_up = jnp.einsum("td,tf->df", hidden_in, pre_grad, preferred_element_type=jnp.float32)
    grad_up_bias = jnp.sum(pre_grad.astype(jnp.float32), axis=0)
    mid_grad = jnp.einsum("tf,df->td", pre_grad, w_up, preferred_element_type=jnp.float32)
    grad_gain_two = jnp.sum(mid_grad * normed_two, axis=0)
    grad_shift_two = jnp.sum(mid_grad, axis=0)
    middle_grad = upstream + norm_back(
        mid_grad, normed_two, inv_two, norm2_gain.astype(jnp.float32)
    )
    branch_grad = middle_grad.astype(jnp.bfloat16)
    grad_out = jnp.einsum("td,te->de", attended, branch_grad, preferred_element_type=jnp.float32)
    grad_out_bias = jnp.sum(branch_grad.astype(jnp.float32), axis=0)
    attended_grad = jnp.einsum(
        "te,de->td", branch_grad, w_out, preferred_element_type=jnp.float32
    ).astype(jnp.bfloat16)
    query_grad, key_grad, value_grad = attention_backward(
        queries,
        key_vecs,
        values,
        attended_grad.reshape(queries.shape),
        log_totals,
        seg_row,
        live_cells,
        block_rows,
    )
    query_grad = query_grad.reshape(length, -1)
    value_grad = value_grad.reshape(length, -1)
    proj_grad = jnp.concatenate([query_grad, key_grad.reshape(length, -1), value_grad], axis=1)
    grad_qkv = jnp.einsum("td,te->de", normed_in, proj_grad, preferred_element_type=jnp.float32)
    grad_query_bias = jnp.sum(query_grad.astype(jnp.float32), axis=0)
    grad_value_bias = jnp.sum(value_grad.astype(jnp.float32), axis=0)
    in_grad = jnp.einsum("te,de->td", proj_grad, w_qkv, preferred_element_type=jnp.float32)
    grad_gain_one = jnp.sum(in_grad * normed_one, axis=0)
    grad_shift_one = jnp.sum(in_grad, axis=0)
    input_grad = (
        middle_grad + norm_back(in_grad, normed_one, inv_one, norm1_gain.astype(jnp.float32))
    ).astype(jnp.bfloat16)
    grads = (
        grad_qkv,
        grad_query_bias,
        grad_value_bias,
        grad_out,
        grad_out_bias,
        grad_up,
        grad_up_bias,
        grad_down,
        grad_down_bias,
        grad_gain_one,
        grad_shift_one,
        grad_gain_two,
        grad_shift_two,
    )
    return (input_grad, grads)


def on_device(
    cell_input,
    cotangent,
    segment_ids,
    lengths,
    w_qkv,
    query_bias,
    value_bias,
    w_out,
    out_bias,
    w_up,
    up_bias,
    w_down,
    down_bias,
    norm1_gain,
    norm1_bias,
    norm2_gain,
    norm2_bias,
):
    shards = (
        w_qkv,
        query_bias,
        value_bias,
        w_out,
        out_bias,
        w_up,
        up_bias,
        w_down,
        down_bias,
        norm1_gain,
        norm1_bias,
        norm2_gain,
        norm2_bias,
    )
    gathered = (
        lax.all_gather(w_qkv, "dp", axis=0, tiled=True),
        lax.all_gather(query_bias, "dp", axis=0, tiled=True),
        lax.all_gather(value_bias, "dp", axis=0, tiled=True),
        lax.all_gather(w_out, "dp", axis=0, tiled=True),
        lax.all_gather(out_bias, "dp", axis=0, tiled=True),
        lax.all_gather(w_up, "dp", axis=0, tiled=True),
        lax.all_gather(up_bias, "dp", axis=0, tiled=True),
        lax.all_gather(w_down, "dp", axis=0, tiled=True),
        lax.all_gather(down_bias, "dp", axis=0, tiled=True),
        lax.all_gather(norm1_gain, "dp", axis=0, tiled=True),
        lax.all_gather(norm1_bias, "dp", axis=0, tiled=True),
        lax.all_gather(norm2_gain, "dp", axis=0, tiled=True),
        lax.all_gather(norm2_bias, "dp", axis=0, tiled=True),
    )
    length, model_width = cell_input.shape
    block_rows = min(length, 512)
    seg_row = segment_ids[0]
    live_cells = jnp.arange(length, dtype=jnp.int32) < lengths[0]
    pos_table = positions(length, model_width)
    block_out, first_kept = forward_pass(
        gathered, cell_input, pos_table, seg_row, live_cells, block_rows
    )
    regathered = (
        lax.all_gather(shards[0], "dp", axis=0, tiled=True),
        lax.all_gather(shards[1], "dp", axis=0, tiled=True),
        lax.all_gather(shards[2], "dp", axis=0, tiled=True),
        lax.all_gather(shards[3], "dp", axis=0, tiled=True),
        lax.all_gather(shards[4], "dp", axis=0, tiled=True),
        lax.all_gather(shards[5], "dp", axis=0, tiled=True),
        lax.all_gather(shards[6], "dp", axis=0, tiled=True),
        lax.all_gather(shards[7], "dp", axis=0, tiled=True),
        lax.all_gather(shards[8], "dp", axis=0, tiled=True),
        lax.all_gather(shards[9], "dp", axis=0, tiled=True),
        lax.all_gather(shards[10], "dp", axis=0, tiled=True),
        lax.all_gather(shards[11], "dp", axis=0, tiled=True),
        lax.all_gather(shards[12], "dp", axis=0, tiled=True),
    )
    recomputed_out, kept = forward_pass(
        regathered, cell_input, pos_table, seg_row, live_cells, block_rows
    )
    input_grad, grads = backward_pass(regathered, kept, cotangent, seg_row, live_cells, block_rows)
    partial_sums = (
        lax.psum_scatter(grads[0], "dp", scatter_dimension=0, tiled=True),
        lax.psum_scatter(grads[1], "dp", scatter_dimension=0, tiled=True),
        lax.psum_scatter(grads[2], "dp", scatter_dimension=0, tiled=True),
        lax.psum_scatter(grads[3], "dp", scatter_dimension=0, tiled=True),
        lax.psum_scatter(grads[4], "dp", scatter_dimension=0, tiled=True),
        lax.psum_scatter(grads[5], "dp", scatter_dimension=0, tiled=True),
        lax.psum_scatter(grads[6], "dp", scatter_dimension=0, tiled=True),
        lax.psum_scatter(grads[7], "dp", scatter_dimension=0, tiled=True),
        lax.psum_scatter(grads[8], "dp", scatter_dimension=0, tiled=True),
        lax.psum_scatter(grads[9], "dp", scatter_dimension=0, tiled=True),
        lax.psum_scatter(grads[10], "dp", scatter_dimension=0, tiled=True),
        lax.psum_scatter(grads[11], "dp", scatter_dimension=0, tiled=True),
        lax.psum_scatter(grads[12], "dp", scatter_dimension=0, tiled=True),
    )
    summed = (
        lax.psum(partial_sums[0].astype(jnp.bfloat16), "rep").astype(jnp.float32),
        lax.psum(partial_sums[1].astype(jnp.bfloat16), "rep").astype(jnp.float32),
        lax.psum(partial_sums[2].astype(jnp.bfloat16), "rep").astype(jnp.float32),
        lax.psum(partial_sums[3].astype(jnp.bfloat16), "rep").astype(jnp.float32),
        lax.psum(partial_sums[4].astype(jnp.bfloat16), "rep").astype(jnp.float32),
        lax.psum(partial_sums[5].astype(jnp.bfloat16), "rep").astype(jnp.float32),
        lax.psum(partial_sums[6].astype(jnp.bfloat16), "rep").astype(jnp.float32),
        lax.psum(partial_sums[7].astype(jnp.bfloat16), "rep").astype(jnp.float32),
        lax.psum(partial_sums[8].astype(jnp.bfloat16), "rep").astype(jnp.float32),
        lax.psum(partial_sums[9].astype(jnp.bfloat16), "rep").astype(jnp.float32),
        lax.psum(partial_sums[10].astype(jnp.bfloat16), "rep").astype(jnp.float32),
        lax.psum(partial_sums[11].astype(jnp.bfloat16), "rep").astype(jnp.float32),
        lax.psum(partial_sums[12].astype(jnp.bfloat16), "rep").astype(jnp.float32),
    )
    return (block_out, input_grad) + tuple(summed)


def solution(mesh):
    in_specs = (
        P(("dp", "rep"), None),
        P(("dp", "rep"), None),
        P(("dp", "rep"), None),
        P(("dp", "rep")),
        P("dp", None),
        P("dp"),
        P("dp"),
        P("dp", None),
        P("dp"),
        P("dp", None),
        P("dp"),
        P("dp", None),
        P("dp"),
        P("dp"),
        P("dp"),
        P("dp"),
        P("dp"),
    )
    out_specs = (
        P(("dp", "rep"), None),
        P(("dp", "rep"), None),
        P("dp", None),
        P("dp"),
        P("dp"),
        P("dp", None),
        P("dp"),
        P("dp", None),
        P("dp"),
        P("dp", None),
        P("dp"),
        P("dp"),
        P("dp"),
        P("dp"),
        P("dp"),
    )
    return jax.shard_map(
        on_device, mesh=mesh, in_specs=in_specs, out_specs=out_specs, check_vma=False
    )
```

profile of v0, /device:TPU:0, one launch (start us, length us, event | category | flops | bytes accessed | tf_op | source)
XLA Modules:
  0.0 1386.3 jit_solution(1670167245353410003)
XLA Ops:
  10.7 1.4 convert_reduce_fusion.1
  12.1 1.6 fusion.37
  13.8 22.9 %all-gather = bf16[8,1,128]{2,1,0:T(2,128)(2,1)S(1)} all-gather(bf16[1,1,128]{2,1,0:T(2,128)(2,1)} %bitcast.104), channel_id=1, replica_groups=mesh['dp'=8,'rep'=4] {'dp'}, dimensions={0}, use_global_device_ids=true | all-gather | bytes 2304 | tf_op jit(solution)/shard_map/all_gather | solution.py:335
  36.8 17.1 %all-gather.1 = bf16[8,1,128]{2,1,0:T(2,128)(2,1)S(1)} all-gather(bf16[1,1,128]{2,1,0:T(2,128)(2,1)} %bitcast.105), channel_id=1, replica_groups=mesh['dp'=8,'rep'=4] {'dp'}, dimensions={0}, use_global_device_ids=true | all-gather | bytes 2304 | tf_op jit(solution)/shard_map/all_gather | solution.py:336
  53.8 3.7 fusion.48
  57.7 2.4 copy.62
  60.2 3.7 reshape.270
  63.9 1.9 copy.63
  65.9 1.5 fusion.30
  67.4 19.0 %all-gather.3 = bf16[8,1,128]{2,1,0:T(2,128)(2,1)S(1)} all-gather(bf16[1,1,128]{2,1,0:T(2,128)(2,1)S(1)} %bitcast.106), channel_id=1, replica_groups=mesh['dp'=8,'rep'=4] {'dp'}, dimensions={0}, use_global_device_ids=true | all-gather | bytes 2304 | tf_op jit(solution)/shard_map/all_gather | solution.py:327
  86.4 16.8 %all-gather.2 = bf16[8,1,128]{2,1,0:T(2,128)(2,1)S(1)} all-gather(bf16[1,1,128]{2,1,0:T(2,128)(2,1)S(1)} %bitcast.107), channel_id=1, replica_groups=mesh['dp'=8,'rep'=4] {'dp'}, dimensions={0}, use_global_device_ids=true | all-gather | bytes 2304 | tf_op jit(solution)/shard_map/all_gather | solution.py:328
  103.2 18.4 %all-gather.4 = bf16[8,1,128]{2,1,0:T(2,128)(2,1)S(1)} all-gather(bf16[1,1,128]{2,1,0:T(2,128)(2,1)S(1)} %bitcast.108), channel_id=1, replica_groups=mesh['dp'=8,'rep'=4] {'dp'}, dimensions={0}, use_global_device_ids=true | all-gather | bytes 2304 | tf_op jit(solution)/shard_map/all_gather | solution.py:330
  121.6 16.4 %all-gather.5 = bf16[8,1,128]{2,1,0:T(2,128)(2,1)S(1)} all-gather(bf16[1,1,128]{2,1,0:T(2,128)(2,1)S(1)} %bitcast.109), channel_id=1, replica_groups=mesh['dp'=8,'rep'=4] {'dp'}, dimensions={0}, use_global_device_ids=true | all-gather | bytes 2304 | tf_op jit(solution)/shard_map/all_gather | solution.py:337
  138.1 18.7 %all-gather.6 = bf16[8,1,128]{2,1,0:T(2,128)(2,1)S(1)} all-gather(bf16[1,1,128]{2,1,0:T(2,128)(2,1)S(1)} %bitcast.110), channel_id=1, replica_groups=mesh['dp'=8,'rep'=4] {'dp'}, dimensions={0}, use_global_device_ids=true | all-gather | bytes 2304 | tf_op jit(solution)/shard_map/all_gather | solution.py:338
  156.7 26.9 %all-gather.7 = bf16[8,1,512]{2,1,0:T(2,128)(2,1)S(1)} all-gather(bf16[1,1,512]{2,1,0:T(2,128)(2,1)S(1)} %reshape.291), channel_id=1, replica_groups=mesh['dp'=8,'rep'=4] {'dp'}, dimensions={0}, use_global_device_ids=true | all-gather | bytes 9216 | tf_op jit(solution)/shard_map/all_gather | solution.py:332
  184.0 5.8 fusion.59
  189.8 1.1 slice.26
  190.9 1.6 fusion.39
  193.1 1.9 copy.66
  195.0 2.7 copy.64
  197.6 7.4 fusion.57
  205.0 8.4 fusion
  213.4 9.2 fusion.41
  222.5 3.3 fusion.58
  226.2 60.7 %all-gather.18.cloned.1.call-done = bf16[1024,4096]{1,0:T(8,128)(2,1)} async-done(((bf16[128,4096]{1,0:T(8,128)(2,1)}), bf16[1024,4096]{1,0:T(8,128)(2,1)}) %all-gather.18.cloned.1.call-update) | async-done | bytes 8388624 | tf_op jit(solution)/shard_map/all_gather | solution.py:331
  286.9 27.3 %fusion.4 = (bf16[512,4096]{1,0:T(8,128)(2,1)}, f32[512,4096]{1,0:T(8,128)}) fusion(f32[4096]{0:T(1024)S(1)} %bitcast.98, bf16[1024,4096]{1,0:T(8,128)(2,1)} %all-gather.18.cloned.1.call-done, f32[512,1024]{1,0:T(8,128)S(1)} %get-tuple-element.133, f32[1024]{0:T(1024)S(1)} %bitcast.102, f32[1024]{0:T(1024)S(1)} %bitcast.91, f32[512]{0:T(512)S(1)} %add_rsqrt_fusion, ...), kind=kOutput, calls=%fused_computation.12 | convolution fusion | flops 4436000768 | bytes 23097344 | tf_op jit(solution)/shard_map/dot_general | solution.py:173
  314.1 97.4 %all-gather.20.cloned.1.call-done = bf16[4096,1024]{1,0:T(8,128)(2,1)} async-done(((bf16[512,1024]{1,0:T(8,128)(2,1)}), bf16[4096,1024]{1,0:T(8,128)(2,1)}) %all-gather.20.cloned.1.call-update) | async-done | bytes 8388624 | tf_op jit(solution)/shard_map/all_gather | solution.py:333
  411.5 11.8 convert_reduce_fusion
  423.4 5.5 multiply_reduce_fusion.1
  429.0 2.7 convert_reduce_fusion.3
  431.7 3.2 fusion.52
  435.6 3.8 convolution_convert_fusion
  439.5 1.9 copy.68
  441.4 14.7 %multiply_reduce_fusion = (f32[16,512]{1,0:T(8,128)}, f32[16,512,512]{1,2,0:T(8,128)}) fusion(f32[16,512,512]{1,2,0:T(8,128)} %get-tuple-element.131, f32[16,512]{1,0:T(8,128)} %log_add_fusion, bf16[512,16,64]{0,2,1:T(8,128)(2,1)S(1)} %bitcast.75, bf16[512,16,64]{0,2,1:T(8,128)(2,1)} %bitcast.79), kind=kOutput, calls=%fused_computation.1 | convolution fusion | flops 549445632 | bytes 35717120 | tf_op jit(solution)/shard_map/while/body/eval_jaxpr/qhd,khd->hqk/dot_general | solution.py:93
  456.1 1.3 slice-done.2
  457.4 1.3 slice-done.3
  458.7 10.8 multiply_convert_fusion
  469.5 6.3 multiply_convert_fusion.1
  475.8 1.5 convert_reduce_fusion.5
  477.4 9.1 convert_reduce_fusion.4
  486.5 1.0 copy-done.22
  487.5 9.4 fusion.45
  496.9 1.5 copy-done.6
  498.4 10.7 fusion.55
  509.2 1.2 copy-done.19
  510.4 10.5 fusion.60
  523.4 18.3 %all-gather.8 = bf16[8,1,128]{2,1,0:T(2,128)(2,1)S(1)} all-gather(bf16[1,1,128]{2,1,0:T(2,128)(2,1)S(1)} %bitcast.111), channel_id=1, replica_groups=mesh['dp'=8,'rep'=4] {'dp'}, dimensions={0}, use_global_device_ids=true | all-gather | bytes 2304 | tf_op jit(solution)/shard_map/all_gather | solution.py:334
  541.9 9.2 fusion.36
  551.1 36.7 %all-reduce.9 = (bf16[1024]{0:T(1024)(128)(2,1)S(1)}, bf16[1024]{0:T(1024)(128)(2,1)S(1)}, bf16[1024]{0:T(1024)(128)(2,1)S(1)}, bf16[4096]{0:T(1024)(128)(2,1)S(...) all-reduce(f32[1024]{0:T(1024)S(1)} %reduce_sum.209, ...), channel_id=3, replica_groups=mesh['dp'=8,'rep'=4] {'dp'}, use_global_device_ids=true, to_apply=%region_14.15.clone | all-reduce | flops 12288 | bytes 73728
  588.5 6.4 all-reduce.10
  599.6 3.3 fusion.35
  602.9 1.9 convert_element_type.255
  604.8 129.0 %reduce-scatter.5.cloned.1.call-done = f32[128,3072]{1,0:T(8,128)} async-done(((f32[1024,3072]{1,0:T(8,128)}), f32[128,3072]{1,0:T(8,128)}) %reduce-scatter.5.cloned.1.call-update) | async-done | bytes 1572880 | tf_op jit(solution)/shard_map/reduce_scatter | solution.py:368
  733.8 2.4 convert_element_type.247
  736.2 280.7 %reduce-scatter.9.cloned.1.call-done = f32[128,4096]{1,0:T(8,128)} async-done(((f32[1024,4096]{1,0:T(8,128)}), f32[128,4096]{1,0:T(8,128)}) %reduce-scatter.9.cloned.1.call-update) | async-done | bytes 2097168 | tf_op jit(solution)/shard_map/reduce_scatter | solution.py:373
  1016.9 2.7 convert_element_type.260
  1019.6 280.4 %reduce-scatter.11.cloned.1.call-done = f32[512,1024]{1,0:T(8,128)} async-done(((f32[4096,1024]{1,0:T(8,128)}), f32[512,1024]{1,0:T(8,128)}) %reduce-scatter.11.cloned.1.call-update) | async-done | bytes 2097168 | tf_op jit(solution)/shard_map/reduce_scatter | solution.py:375
  1300.1 2.7 convert_element_type.265
  1302.8 10.2 add_convert_fusion
  1313.1 57.8 %all-reduce.14.cloned.1.call-done = (bf16[128,3072]{1,0:T(8,128)(2,1)}, bf16[128,1024]{1,0:T(8,128)(2,1)}, bf16[128,4096]{1,0:T(8,128)(2,1)}, bf16[512,1024]{1,0:T(8,128)(2,1)}) async-done(((bf16[128,3072]{1,0:T(8,128)(2,1)}, bf16[128,1024]{1,0:T(8,128)(2,1)}, bf16[128,4096]{1,0:T(8,128)(2,1)}, bf16[512,1024]{1,0:T(8,128)(2,1)}), (bf16[128,3072]{1,0:T(8,128)(2,1)}, bf16[128,1024]{1,0:T(8,128)(2,1)}, ...) | async-done | bytes 3145744 | tf_op jit(solution)/shard_map/psum | solution.py:383
  1370.9 1.9 convert_element_type.256
  1372.8 2.4 convert_element_type.248
  1375.2 2.8 convert_element_type.261
  1377.9 1.6 convert_element_type.266
  (172 shorter events, 12.1 us)
Async XLA Ops:
  7.2 176.8 %all-gather.14.cloned.1.call-start = ((), (), s32[]{:S(2)}) async-start(), calls=%async_computation.4 | async-start | bytes 7077888 | tf_op jit(solution)/shard_map/all_gather | solution.py:326
  7.9 214.6 %all-gather.16.cloned.1.call-start = ((), (), s32[]{:S(2)}) async-start(), calls=%async_computation.5 | async-start | bytes 2359296 | tf_op jit(solution)/shard_map/all_gather | solution.py:329
  8.7 278.2 %all-gather.18.cloned.1.call-start = ((), (), s32[]{:S(2)}) async-start(), calls=%async_computation.6 | async-start | bytes 9437184 | tf_op jit(solution)/shard_map/all_gather | solution.py:331
  9.4 402.1 %all-gather.20.cloned.1.call-start = ((), (), s32[]{:S(2)}) async-start(), calls=%async_computation.7 | async-start | bytes 9437184 | tf_op jit(solution)/shard_map/all_gather | solution.py:333
  10.0 592.9 %reduce-scatter.7.cloned.1.call-start = ((), (), s32[]{:S(2)}) async-start(), calls=%async_computation.9 | async-start | bytes 4718592 | tf_op jit(solution)/shard_map/reduce_scatter | solution.py:371
  12.1 53.7 %copy-start.27 = (f32[512]{0:T(512)}, f32[512]{0:T(512)S(1)}, u32[]{:S(2)}) copy-start(f32[512]{0:T(512)S(1)} %broadcast_multiply_fusion.5) | copy-start | bytes 6148
  13.8 52.1 %copy-start.29 = (f32[512]{0:T(512)}, f32[512]{0:T(512)S(1)}, u32[]{:S(2)}) copy-start(f32[512]{0:T(512)S(1)} %add_rsqrt_fusion.1) | copy-start | bytes 6148
  36.8 29.1 %copy-start.25 = (f32[8,1,128]{2,1,0:T(1,128)}, f32[8,1,128]{2,1,0:T(1,128)S(1)}, u32[]{:S(2)}) copy-start(f32[8,1,128]{2,1,0:T(1,128)S(1)} %convert_element_type.277) | copy-start | bytes 12292
  57.7 8.2 copy-start.1
  60.2 7.2 copy-start.41
  60.2 7.2 copy-start.42
  60.2 26.2 %copy-start.43 = (bf16[128]{0:T(256)(128)(2,1)S(1)}, bf16[128]{0:T(256)(128)(2,1)}, u32[]{:S(2)}) copy-start(bf16[128]{0:T(256)(128)(2,1)} %param.23) | copy-start | bytes 772
  60.2 43.0 %copy-start.44 = (bf16[128]{0:T(256)(128)(2,1)S(1)}, bf16[128]{0:T(256)(128)(2,1)}, u32[]{:S(2)}) copy-start(bf16[128]{0:T(256)(128)(2,1)} %param.25) | copy-start | bytes 772
  60.2 61.4 %copy-start.45 = (bf16[128]{0:T(256)(128)(2,1)S(1)}, bf16[128]{0:T(256)(128)(2,1)}, u32[]{:S(2)}) copy-start(bf16[128]{0:T(256)(128)(2,1)} %param.32) | copy-start | bytes 772
  60.2 77.9 %copy-start.46 = (bf16[128]{0:T(256)(128)(2,1)S(1)}, bf16[128]{0:T(256)(128)(2,1)}, u32[]{:S(2)}) copy-start(bf16[128]{0:T(256)(128)(2,1)} %param.33) | copy-start | bytes 772
  60.2 123.4 %copy-start.34 = (s32[1,512]{1,0:T(1,128)S(1)}, s32[1,512]{1,0:T(1,128)}, u32[]{:S(2)}) copy-start(s32[1,512]{1,0:T(1,128)} %param.19) | copy-start | bytes 6148
  138.1 290.9 %copy-start.31 = (f32[8,1,128]{2,1,0:T(1,128)}, f32[8,1,128]{2,1,0:T(1,128)S(1)}, u32[]{:S(2)}) copy-start(f32[8,1,128]{2,1,0:T(1,128)S(1)} %convert_element_type.282) | copy-start | bytes 12292
  156.7 130.1 %copy-start.39 = (f32[8,1,128]{2,1,0:T(1,128)}, f32[8,1,128]{2,1,0:T(1,128)S(1)}, u32[]{:S(2)}) copy-start(f32[8,1,128]{2,1,0:T(1,128)S(1)} %convert_element_type.283) | copy-start | bytes 12292
  193.0 11.9 copy-start.10
  194.9 10.1 copy-start.8
  205.0 8.4 copy-start.15
  225.8 197.6 %copy-start.5 = (f32[512,1024]{1,0:T(8,128)}, f32[512,1024]{1,0:T(8,128)S(1)}, u32[]{:S(2)}) copy-start(f32[512,1024]{1,0:T(8,128)S(1)} %get-tuple-element.133) | copy-start | bytes 6291460
  226.2 202.8 %copy-start.35 = (f32[512]{0:T(512)}, f32[512]{0:T(512)S(1)}, u32[]{:S(2)}) copy-start(f32[512]{0:T(512)S(1)} %add_rsqrt_fusion) | copy-start | bytes 6148
  286.9 124.7 %copy-start.17 = (bf16[512,1024]{1,0:T(8,128)(2,1)S(1)}, bf16[512,1024]{1,0:T(8,128)(2,1)}, u32[]{:S(2)}) copy-start(bf16[512,1024]{1,0:T(8,128)(2,1)} %param.18) | copy-start | bytes 3145732
  411.5 11.9 copy-start.48
  423.4 5.6 copy-start.50
  423.4 5.6 copy-start.18
  428.9 2.7 copy-start.14
  431.7 4.0 copy-start.3
  435.0 298.8 %reduce-scatter.5.cloned.1.call-start = ((), (), s32[]{:S(2)}) async-start(), calls=%async_computation.8 | async-start | bytes 14155776 | tf_op jit(solution)/shard_map/reduce_scatter | solution.py:368
  441.4 14.8 %copy-start.12 = (bf16[512,1024]{0,1:T(8,128)(2,1)}, bf16[512,1024]{0,1:T(8,128)(2,1)S(1)}, u32[]{:S(2)}) copy-start(bf16[512,1024]{0,1:T(8,128)(2,1)S(1)} %copy.68) | copy-start | bytes 3145732
  441.4 14.8 %slice-start = ((s8[16777216]{0:T(1024)(128)(4,1)}), s8[4194304]{0:T(1024)(128)(4,1)S(1)}, s32[]{:S(2)}) async-start(s8[16777216]{0:T(1024)(128)(4,1)} %bitcast.69), calls=%async_computation.13 | async-start | bytes 8388608
  441.4 14.7 %slice-start.1 = ((s8[16777216]{0:T(1024)(128)(4,1)}), s8[4194304]{0:T(1024)(128)(4,1)S(1)}, s32[]{:S(2)}) async-start(s8[16777216]{0:T(1024)(128)(4,1)} %bitcast.69), calls=%async_computation.14 | async-start | bytes 8388608
  441.4 16.0 %slice-start.2 = ((s8[16777216]{0:T(1024)(128)(4,1)}), s8[4194304]{0:T(1024)(128)(4,1)S(1)}, s32[]{:S(2)}) async-start(s8[16777216]{0:T(1024)(128)(4,1)} %bitcast.69), calls=%async_computation.15 | async-start | bytes 8388608
  441.4 17.3 %slice-start.3 = ((s8[16777216]{0:T(1024)(128)(4,1)}), s8[4194304]{0:T(1024)(128)(4,1)S(1)}, s32[]{:S(2)}) async-start(s8[16777216]{0:T(1024)(128)(4,1)} %bitcast.69), calls=%async_computation.16 | async-start | bytes 8388608
  458.7 10.8 copy-start.11
  469.5 6.3 copy-start
  469.5 6.3 copy-start.9
  475.8 10.7 copy-start.21
  475.8 1.6 copy-start.13
  475.8 1.6 copy-start.24
  477.4 9.1 copy-start.16
  477.4 10.1 copy-start.20
  486.5 1.0 copy-start.22
  496.8 1.6 copy-start.6
  496.8 1.6 copy-start.32
  496.9 1.6 copy-start.36
  496.9 1.6 copy-start.40
  496.9 520.0 %reduce-scatter.9.cloned.1.call-start = ((), (), s32[]{:S(2)}) async-start(), calls=%async_computation.10 | async-start | bytes 18874368 | tf_op jit(solution)/shard_map/reduce_scatter | solution.py:373
  509.2 1.2 copy-start.19
  509.2 790.9 %reduce-scatter.11.cloned.1.call-start = ((), (), s32[]{:S(2)}) async-start(), calls=%async_computation.11 | async-start | bytes 18874368 | tf_op jit(solution)/shard_map/reduce_scatter | solution.py:375
  520.9 0.7 copy-start.49
  520.9 2.5 copy-start.47
  520.9 21.0 %copy-start.2 = (bf16[512,1024]{1,0:T(8,128)(2,1)S(1)}, bf16[512,1024]{1,0:T(8,128)(2,1)}, u32[]{:S(2)}) copy-start(bf16[512,1024]{1,0:T(8,128)(2,1)} %param.17) | copy-start | bytes 3145732
  520.9 21.0 %copy-start.26 = (f32[8,1,128]{2,1,0:T(1,128)S(1)}, f32[8,1,128]{2,1,0:T(1,128)}, u32[]{:S(2)}) copy-start(f32[8,1,128]{2,1,0:T(1,128)} %copy-done.25) | copy-start | bytes 12292
  520.9 21.0 %copy-start.28 = (f32[512]{0:T(512)S(1)}, f32[512]{0:T(512)}, u32[]{:S(2)}) copy-start(f32[512]{0:T(512)} %copy-done.27) | copy-start | bytes 6148
  520.9 21.0 %copy-start.30 = (f32[512]{0:T(512)S(1)}, f32[512]{0:T(512)}, u32[]{:S(2)}) copy-start(f32[512]{0:T(512)} %copy-done.29) | copy-start | bytes 6148
  520.9 849.9 %all-reduce.14.cloned.1.call-start = ((), (), s32[]{:S(2)}) async-start(), calls=%async_computation.12 | async-start | bytes 6291456 | tf_op jit(solution)/shard_map/psum | solution.py:383
  541.9 9.2 copy-start.33
  541.9 9.2 copy-start.37
  541.9 9.2 copy-start.38
  541.9 57.7 %copy-start.4 = (f32[512,1024]{1,0:T(8,128)S(1)}, f32[512,1024]{1,0:T(8,128)}, u32[]{:S(2)}) copy-start(f32[512,1024]{1,0:T(8,128)} %copy-done.3) | copy-start | bytes 6291460
  602.9 700.0 %copy-start.7 = (f32[512,1024]{1,0:T(8,128)S(1)}, f32[512,1024]{1,0:T(8,128)}, u32[]{:S(2)}) copy-start(f32[512,1024]{1,0:T(8,128)} %copy-done.5) | copy-start | bytes 6291460
  1370.9 7.1 copy-start.23
Sparse Core Ops, SparseCore 0:
  10.2 101.6 all-gather.13
  114.0 47.6 all-gather.15
  163.8 123.0 all-gather.17
  288.9 122.6 all-gather.19
  435.1 86.6 reduce-scatter.6
  525.2 208.5 reduce-scatter.4
  737.6 279.3 reduce-scatter.8
  1020.7 279.3 reduce-scatter.10
  1303.2 67.5 all-reduce.13
where the time goes:
time: 1390 us
  waiting for transfers between devices  909 us (65%)
  blocking collectives  218 us (16%)
  matrix products  159 us (11%)
  other arithmetic  59.6 us (4%)
  local copies, waits for them, and re-layouts  24.6 us (2%)
  between operations  16.6 us (1%)
    reduce_scatter x1, waiting for transfers between devices, on_device(): lax.psum_scatter(grads[5], 'dp', scatter_dimension=0, tiled=True)  281 us
    reduce_scatter x1, waiting for transfers between devices, on_device(): lax.psum_scatter(grads[7], 'dp', scatter_dimension=0, tiled=True)  280 us
    reduce_scatter x1, waiting for transfers between devices, on_device(): lax.psum_scatter(grads[0], 'dp', scatter_dimension=0, tiled=True)  129 us
    all_gather x1, waiting for transfers between devices, on_device(): lax.all_gather(w_down, 'dp', axis=0, tiled=True)  97.4 us
    all_gather x1, waiting for transfers between devices, on_device(): lax.all_gather(w_up, 'dp', axis=0, tiled=True)  60.7 us
    psum x1, waiting for transfers between devices, on_device(): lax.psum(partial_sums[0].astype(jnp.bfloat16), 'rep').astype(jnp.float32)  57.8 us
    unnamed x1, blocking collectives  36.7 us
  transfers between devices with their start and end apart: 9, of which 6 were waited for; matrix products, arithmetic and copies ran while one was open for 15% of the time, Pallas kernels for 0%

commit v1 on v0

--- a/solution.py
+++ b/solution.py
@@ -288,112 +288,71 @@
     return (input_grad, grads)
 
 
+VECTORS = (1, 2, 4, 6, 8, 9, 10, 11, 12)
+MATRICES = (0, 3, 5, 7)
+EVERY = ("dp", "rep")
+
+
+def gather_matrix(shard):
+    part_rows = shard.shape[0] // lax.axis_size("rep")
+    own = lax.dynamic_slice_in_dim(shard, lax.axis_index("rep") * part_rows, part_rows, 0)
+    return lax.all_gather(own, EVERY, axis=0, tiled=True)
+
+
+def gather_vectors(shards):
+    packed = jnp.concatenate(shards)
+    whole = lax.all_gather(packed, "dp", axis=0, tiled=False)
+    vectors, begin = [], 0
+    for shard in shards:
+        vectors.append(whole[:, begin : begin + shard.shape[0]].reshape(-1))
+        begin += shard.shape[0]
+    return vectors
+
+
+def reduce_matrix(grad):
+    part = lax.psum_scatter(grad.astype(jnp.bfloat16), EVERY, scatter_dimension=0, tiled=True)
+    return lax.all_gather(part, "rep", axis=0, tiled=True).astype(jnp.float32)
+
+
+def reduce_vectors(grads):
+    owners = lax.axis_size("dp")
+    packed = jnp.concatenate([grad.reshape(owners, -1) for grad in grads], axis=1)
+    total = lax.psum(packed, EVERY)
+    own = lax.dynamic_index_in_dim(total, lax.axis_index("dp"), 0, keepdims=False)
+    outs, begin = [], 0
+    for grad in grads:
+        size = grad.shape[0] // owners
+        outs.append(own[begin : begin + size])
+        begin += size
+    return outs
+
+
 def on_device(
     cell_input,
     cotangent,
     segment_ids,
     lengths,
-    w_qkv,
-    query_bias,
-    value_bias,
-    w_out,
-    out_bias,
-    w_up,
-    up_bias,
-    w_down,
-    down_bias,
-    norm1_gain,
-    norm1_bias,
-    norm2_gain,
-    norm2_bias,
+    *shards,
 ):
-    shards = (
-        w_qkv,
-        query_bias,
-        value_bias,
-        w_out,
-        out_bias,
-        w_up,
-        up_bias,
-        w_down,
-        down_bias,
-        norm1_gain,
-        norm1_bias,
-        norm2_gain,
-        norm2_bias,
-    )
-    gathered = (
-        lax.all_gather(w_qkv, "dp", axis=0, tiled=True),
-        lax.all_gather(query_bias, "dp", axis=0, tiled=True),
-        lax.all_gather(value_bias, "dp", axis=0, tiled=True),
-        lax.all_gather(w_out, "dp", axis=0, tiled=True),
-        lax.all_gather(out_bias, "dp", axis=0, tiled=True),
-        lax.all_gather(w_up, "dp", axis=0, tiled=True),
-        lax.all_gather(up_bias, "dp", axis=0, tiled=True),
-        lax.all_gather(w_down, "dp", axis=0, tiled=True),
-        lax.all_gather(down_bias, "dp", axis=0, tiled=True),
-        lax.all_gather(norm1_gain, "dp", axis=0, tiled=True),
-        lax.all_gather(norm1_bias, "dp", axis=0, tiled=True),
-        lax.all_gather(norm2_gain, "dp", axis=0, tiled=True),
-        lax.all_gather(norm2_bias, "dp", axis=0, tiled=True),
-    )
+    gathered = [None] * len(shards)
+    for place, vector in zip(VECTORS, gather_vectors([shards[place] for place in VECTORS])):
+        gathered[place] = vector
+    for place in MATRICES:
+        gathered[place] = gather_matrix(shards[place])
     length, model_width = cell_input.shape
     block_rows = min(length, 512)
     seg_row = segment_ids[0]
     live_cells = jnp.arange(length, dtype=jnp.int32) < lengths[0]
     pos_table = positions(length, model_width)
-    block_out, first_kept = forward_pass(
+    block_out, kept = forward_pass(
         gathered, cell_input, pos_table, seg_row, live_cells, block_rows
     )
-    regathered = (
-        lax.all_gather(shards[0], "dp", axis=0, tiled=True),
-        lax.all_gather(shards[1], "dp", axis=0, tiled=True),
-        lax.all_gather(shards[2], "dp", axis=0, tiled=True),
-        lax.all_gather(shards[3], "dp", axis=0, tiled=True),
-        lax.all_gather(shards[4], "dp", axis=0, tiled=True),
-        lax.all_gather(shards[5], "dp", axis=0, tiled=True),
-        lax.all_gather(shards[6], "dp", axis=0, tiled=True),
-        lax.all_gather(shards[7], "dp", axis=0, tiled=True),
-        lax.all_gather(shards[8], "dp", axis=0, tiled=True),
-        lax.all_gather(shards[9], "dp", axis=0, tiled=True),
-        lax.all_gather(shards[10], "dp", axis=0, tiled=True),
-        lax.all_gather(shards[11], "dp", axis=0, tiled=True),
-        lax.all_gather(shards[12], "dp", axis=0, tiled=True),
-    )
-    recomputed_out, kept = forward_pass(
-        regathered, cell_input, pos_table, seg_row, live_cells, block_rows
-    )
-    input_grad, grads = backward_pass(regathered, kept, cotangent, seg_row, live_cells, block_rows)
-    partial_sums = (
-        lax.psum_scatter(grads[0], "dp", scatter_dimension=0, tiled=True),
-        lax.psum_scatter(grads[1], "dp", scatter_dimension=0, tiled=True),
-        lax.psum_scatter(grads[2], "dp", scatter_dimension=0, tiled=True),
-        lax.psum_scatter(grads[3], "dp", scatter_dimension=0, tiled=True),
-        lax.psum_scatter(grads[4], "dp", scatter_dimension=0, tiled=True),
-        lax.psum_scatter(grads[5], "dp", scatter_dimension=0, tiled=True),
-        lax.psum_scatter(grads[6], "dp", scatter_dimension=0, tiled=True),
-        lax.psum_scatter(grads[7], "dp", scatter_dimension=0, tiled=True),
-        lax.psum_scatter(grads[8], "dp", scatter_dimension=0, tiled=True),
-        lax.psum_scatter(grads[9], "dp", scatter_dimension=0, tiled=True),
-        lax.psum_scatter(grads[10], "dp", scatter_dimension=0, tiled=True),
-        lax.psum_scatter(grads[11], "dp", scatter_dimension=0, tiled=True),
-        lax.psum_scatter(grads[12], "dp", scatter_dimension=0, tiled=True),
-    )
-    summed = (
-        lax.psum(partial_sums[0].astype(jnp.bfloat16), "rep").astype(jnp.float32),
-        lax.psum(partial_sums[1].astype(jnp.bfloat16), "rep").astype(jnp.float32),
-        lax.psum(partial_sums[2].astype(jnp.bfloat16), "rep").astype(jnp.float32),
-        lax.psum(partial_sums[3].astype(jnp.bfloat16), "rep").astype(jnp.float32),
-        lax.psum(partial_sums[4].astype(jnp.bfloat16), "rep").astype(jnp.float32),
-        lax.psum(partial_sums[5].astype(jnp.bfloat16), "rep").astype(jnp.float32),
-        lax.psum(partial_sums[6].astype(jnp.bfloat16), "rep").astype(jnp.float32),
-        lax.psum(partial_sums[7].astype(jnp.bfloat16), "rep").astype(jnp.float32),
-        lax.psum(partial_sums[8].astype(jnp.bfloat16), "rep").astype(jnp.float32),
-        lax.psum(partial_sums[9].astype(jnp.bfloat16), "rep").astype(jnp.float32),
-        lax.psum(partial_sums[10].astype(jnp.bfloat16), "rep").astype(jnp.float32),
-        lax.psum(partial_sums[11].astype(jnp.bfloat16), "rep").astype(jnp.float32),
-        lax.psum(partial_sums[12].astype(jnp.bfloat16), "rep").astype(jnp.float32),
-    )
+    input_grad, grads = backward_pass(gathered, kept, cotangent, seg_row, live_cells, block_rows)
+    summed = [None] * len(grads)
+    for place in (7, 5, 3, 0):
+        summed[place] = reduce_matrix(grads[place])
+    for place, vector in zip(VECTORS, reduce_vectors([grads[place] for place in VECTORS])):
+        summed[place] = vector
     return (block_out, input_grad) + tuple(summed)
 
 

time: 1390 us -> 921 us (0.66)
  waiting for transfers between devices: 909 us -> 579 us
  blocking collectives: 218 us -> 87.5 us
  other arithmetic: 59.6 us -> 41.1 us
    reduce_scatter x4, waiting for transfers between devices: 690 us -> 396 us  [reduce_matrix(): lax.psum_scatter(grad.astype(jnp.bfloat16), EVERY, scatter_dimension=0, t...]
    all_gather x9 -> x3, blocking collectives: 174 us -> 47.4 us  [the longest x1 32.7 us: gather_vectors(): whole = lax.all_gather(packed, 'dp', axis=0, tiled=False)]
    psum x1 -> x0, waiting for transfers between devices: 57.8 us -> none  [on_device(): lax.psum(partial_sums[0].astype(jnp.bfloat16), 'rep').astype(jnp.float32)]
    unnamed x1 -> x0, blocking collectives: 36.7 us -> none
    psum x1, blocking collectives: 6.38 us -> 40.1 us  [reduce_vectors(): total = lax.psum(packed, EVERY)]
    all_gather x4 -> x6, waiting for transfers between devices: 158 us -> 183 us  [the longest x4 161 us: gather_matrix(): return lax.all_gather(own, EVERY, axis=0, tiled=True)]
    convert_element_type x25 -> x4, other arithmetic: 23.1 us -> 7.68 us  [reduce_matrix(): return lax.all_gather(part, 'rep', axis=0, tiled=True).astype(jnp.float32)]
  transfers between devices with their start and end apart: 9 -> 10, of which waited for: 6 -> 10; matrix products, arithmetic and copies ran while one was open for 15% -> 22% of each run, Pallas kernels for 0% -> 0%
where the time goes in v1:
time: 921 us; the launch traced here: 915 us
  waiting for transfers between devices  579 us (63%)
  matrix products  154 us (17%)
  blocking collectives  87.5 us (10%)
  other arithmetic  41.1 us (4%)
  local copies, waits for them, and re-layouts  36.9 us (4%)
  between operations  15.8 us (2%)
    reduce_scatter x4, waiting for transfers between devices, reduce_matrix(): lax.psum_scatter(grad.astype(jnp.bfloat16), EVERY, scatter_dimension=0, t...  396 us
    all_gather x4, waiting for transfers between devices, gather_matrix(): return lax.all_gather(own, EVERY, axis=0, tiled=True)  161 us
    psum x1, blocking collectives, reduce_vectors(): total = lax.psum(packed, EVERY)  40.1 us
    all_gather x1, blocking collectives, gather_vectors(): whole = lax.all_gather(packed, 'dp', axis=0, tiled=False)  32.7 us
    dot_general x1, matrix products, forward_pass(): jnp.dot(hidden_in, w_up, preferred_element_type=jnp.float32)  27 us
    all_gather x2, waiting for transfers between devices, reduce_matrix(): return lax.all_gather(part, 'rep', axis=0, tiled=True).astype(jnp.float32)  22.6 us
  transfers between devices with their start and end apart: 10, of which 10 were waited for; matrix products, arithmetic and copies ran while one was open for 22% of the time, Pallas kernels for 0%

profile of v1, /device:TPU:0, one launch (start us, length us, event | category | flops | bytes accessed | tf_op | source)
XLA Modules:
  0.0 915.2 jit_solution(13305810542900627797)
XLA Ops:
  7.2 1.7 constant_dynamic-slice_fusion.4
  9.0 1.5 constant_dynamic-slice_fusion.3
  11.4 1.7 constant_dynamic-slice_fusion.1
  13.8 0.9 dynamic-update-slice.9
  14.7 0.8 dynamic-update-slice.10
  15.5 0.8 dynamic-update-slice.11
  16.3 0.9 dynamic-update-slice.12
  17.2 0.8 dynamic-update-slice.13
  18.0 0.8 dynamic-update-slice.14
  19.7 0.8 dynamic-update-slice.16
  21.3 32.7 %all-gather.1 = bf16[8,1,1536]{2,1,0:T(2,128)(2,1)S(1)} all-gather(bf16[1,1,1536]{2,1,0:T(2,128)(2,1)S(1)} %reshape.394), channel_id=2, replica_groups=mesh['dp'=8,'rep'=4] {'dp'}, dimensions={0}, use_global_device_ids=true | all-gather | bytes 27648 | tf_op jit(solution)/shard_map/all_gather | solution.py:304
  54.0 3.7 fusion.47
  58.0 2.6 copy.62
  60.6 3.7 reshape.368
  64.3 1.9 copy.63
  67.8 1.5 fusion.30
  69.3 14.1 %all-gather.9.cloned.1.call-done = bf16[1024,3072]{1,0:T(8,128)(2,1)} async-done(((bf16[32,3072]{1,0:T(8,128)(2,1)}), bf16[1024,3072]{1,0:T(8,128)(2,1)}) %all-gather.9.cloned.1.call-update) | async-done | bytes 6291472 | tf_op jit(solution)/shard_map/all_gather | solution.py:299
  83.4 5.8 fusion.65
  89.2 1.1 slice.165
  90.4 1.6 fusion.39
  92.5 1.9 copy.66
  94.4 2.7 copy.64
  97.1 7.4 fusion.63
  104.4 8.4 fusion
  112.9 8.9 fusion.41
  121.7 19.3 %all-gather.11.cloned.1.call-done = bf16[1024,1024]{1,0:T(8,128)(2,1)} async-done(((bf16[32,1024]{1,0:T(8,128)(2,1)}), bf16[1024,1024]{1,0:T(8,128)(2,1)}) %all-gather.11.cloned.1.call-update) | async-done | bytes 2097168 | tf_op jit(solution)/shard_map/all_gather | solution.py:299
  141.0 3.3 fusion.64
  144.7 75.7 %all-gather.13.cloned.1.call-done = bf16[1024,4096]{1,0:T(8,128)(2,1)} async-done(((bf16[32,4096]{1,0:T(8,128)(2,1)}), bf16[1024,4096]{1,0:T(8,128)(2,1)}) %all-gather.13.cloned.1.call-update) | async-done | bytes 8388624 | tf_op jit(solution)/shard_map/all_gather | solution.py:299
  220.4 27.0 %fusion.4 = (bf16[512,4096]{1,0:T(8,128)(2,1)}, f32[512,4096]{1,0:T(8,128)}) fusion(f32[4096]{0:T(1024)S(1)} %bitcast.148, bf16[1024,4096]{1,0:T(8,128)(2,1)} %all-gather.13.cloned.1.call-done, f32[512,1024]{1,0:T(8,128)S(1)} %get-tuple-element.106, f32[1024]{0:T(1024)S(1)} %get-tuple-element.94, f32[1024]{0:T(1024)S(1)} %get-tuple-element.95, ...), kind=kOutput, calls=%fused_computation.12 | convolution fusion | flops 4436000768 | bytes 23097344 | tf_op jit(solution)/shard_map/dot_general | solution.py:173
  247.4 51.4 %all-gather.15.cloned.1.call-done = bf16[4096,1024]{1,0:T(8,128)(2,1)} async-done(((bf16[128,1024]{1,0:T(8,128)(2,1)}), bf16[4096,1024]{1,0:T(8,128)(2,1)}) %all-gather.15.cloned.1.call-update) | async-done | bytes 8388624 | tf_op jit(solution)/shard_map/all_gather | solution.py:299
  298.8 11.3 %convert_reduce_fusion = (f32[4096]{0:T(1024)}, bf16[512,4096]{1,0:T(8,128)(2,1)S(1)}) fusion(f32[512,4096]{1,0:T(8,128)} %get-tuple-element.108, f32[4096]{0:T(1024)S(1)} %bitcast.149, bf16[4096,1024]{1,0:T(8,128)(2,1)} %all-gather.15.cloned.1.call-done, bf16[512,1024]{1,0:T(8,128)(2,1)S(1)} %copy-done.15), kind=kOutput, calls=%fused_computation.20 | convolution fusion | flops 4322226176 | bytes 22052864 | tf_op jit(solution)/shard_map/td,fd->tf/dot_general | solution.py:235
  310.1 2.0 copy-done.30
  312.1 7.3 convolution_convert_fusion.1
  319.5 9.1 convolution_convert_fusion
  329.3 9.4 %multiply_reduce_fusion.1 = (f32[1024]{0:T(1024)}, f32[512]{0:T(512)S(1)}, f32[512]{0:T(512)S(1)}, f32[1024]{0:T(1024)S(1)}, f32[512,1024]{1,0:T(8,128)S(1)}) fusion(f32[512,1024]{1,0:T(8,128)S(1)} %get-tuple-element.106, f32[512]{0:T(512)S(1)} %add_rsqrt_fusion, f32[512]{0:T(512)S(1)} %broadcast_multiply_fusion.4, f32[1024]{0:T(1024)S(1)} %get-tuple-element.95, ...), kind=kOutput, calls=%fused_computation.70 | convolution fusion | flops 4299682816 | bytes 16797696 | tf_op jit(solution)/shard_map/tf,df->td/dot_general | solution.py:239
  338.7 1.0 convert_reduce_fusion.3
  339.7 1.3 copy-done.12
  341.0 1.3 convolution_convert_fusion.4
  342.9 4.6 convolution_convert_fusion.3
  347.6 14.7 %multiply_reduce_fusion = (f32[16,512]{1,0:T(8,128)}, f32[16,512,512]{1,2,0:T(8,128)}) fusion(f32[16,512,512]{1,2,0:T(8,128)} %get-tuple-element.104, f32[16,512]{1,0:T(8,128)} %log_add_fusion, bf16[512,16,64]{0,2,1:T(8,128)(2,1)S(1)} %bitcast.134, bf16[512,16,64]{0,2,1:T(8,128)(2,1)} %bitcast.136), kind=kOutput, calls=%fused_computation.1 | convolution fusion | flops 549445632 | bytes 35717120 | tf_op jit(solution)/shard_map/while/body/eval_jaxpr/qhd,khd->hqk/dot_general | solution.py:93
  362.4 1.0 slice-done.2
  363.4 1.2 slice-done.3
  364.6 10.5 %multiply_convert_fusion = bf16[16,512,512]{1,2,0:T(8,128)(2,1)} fusion(f32[16,512,512]{1,2,0:T(8,128)} %get-tuple-element.111, f32[16,512,512]{1,2,0:T(8,128)S(1)} %bitcast.129, f32[16,512]{1,0:T(8,128)} %get-tuple-element.110, f32[16,512]{1,0:T(8,128)} %log_add_fusion), kind=kLoop, calls=%fused_computation | loop fusion | flops 16777216 | bytes 42008576 | tf_op jit(solution)/shard_map/while/body/eval_jaxpr/convert_element_type | solution.py:98
  375.2 6.6 multiply_convert_fusion.1
  381.8 1.5 convert_reduce_fusion.5
  383.3 8.9 convert_reduce_fusion.4
  392.2 1.0 copy-done.17
  393.1 8.4 convolution_convert_fusion.2
  402.8 8.5 fusion.36
  411.3 57.1 %reduce-scatter.9.cloned.1.call-done = bf16[32,4096]{1,0:T(8,128)(2,1)} async-done(((bf16[1024,4096]{1,0:T(8,128)(2,1)}), bf16[32,4096]{1,0:T(8,128)(2,1)}) %reduce-scatter.9.cloned.1.call-update) | async-done | bytes 262160 | tf_op jit(solution)/shard_map/reduce_scatter | solution.py:313
  468.5 40.1 %psum.7 = f32[8,1536]{1,0:T(8,128)S(1)} all-reduce(f32[8,1536]{1,0:T(8,128)S(1)} %constant_dynamic-update-slice_fusion), channel_id=1, replica_groups=mesh['dp'=8,'rep'=4] {'dp','rep'}, use_global_device_ids=true, to_apply=%region_21.22 | all-reduce | flops 12288 | bytes 98304 | tf_op jit(solution)/shard_map/psum | solution.py:320
  509.9 3.9 fusion.35
  513.9 102.6 %reduce-scatter.11.cloned.1.call-done = bf16[128,1024]{1,0:T(8,128)(2,1)} async-done(((bf16[4096,1024]{1,0:T(8,128)(2,1)}), bf16[128,1024]{1,0:T(8,128)(2,1)}) %reduce-scatter.11.cloned.1.call-update) | async-done | bytes 262160 | tf_op jit(solution)/shard_map/reduce_scatter | solution.py:313
  616.6 10.2 %add_convert_fusion = bf16[512,1024]{1,0:T(8,128)(2,1)} fusion(f32[512,1024]{1,0:T(8,128)S(1)} %copy-done.6, bf16[512,4096]{1,0:T(8,128)(2,1)} %get-tuple-element.107, bf16[4096,1024]{1,0:T(8,128)(2,1)} %all-gather.15.cloned.1.call-done, f32[1024]{0:T(1024)S(1)} %copy-done.28), kind=kOutput, calls=%fused_computation.77 | convolution fusion | flops 4296540160 | bytes 15732736 | tf_op jit(solution)/shard_map/dot_general | solution.py:179
  626.8 126.4 %reduce-scatter.7.cloned.1.call-done = bf16[32,1024]{1,0:T(8,128)(2,1)} async-done(((bf16[1024,1024]{1,0:T(8,128)(2,1)}), bf16[32,1024]{1,0:T(8,128)(2,1)}) %reduce-scatter.7.cloned.1.call-update) | async-done | bytes 65552 | tf_op jit(solution)/shard_map/reduce_scatter | solution.py:313
  753.2 6.0 all_gather.37
  759.1 0.8 convert_element_type.253
  760.0 109.7 %reduce-scatter.5.cloned.1.call-done = bf16[32,3072]{1,0:T(8,128)(2,1)} async-done(((bf16[1024,3072]{1,0:T(8,128)(2,1)}), bf16[32,3072]{1,0:T(8,128)(2,1)}) %reduce-scatter.5.cloned.1.call-update) | async-done | bytes 196624 | tf_op jit(solution)/shard_map/reduce_scatter | solution.py:313
  869.7 8.8 all_gather.36
  878.5 1.3 convert_element_type.247
  879.8 7.2 all-gather.17.cloned.1.call-done
  887.0 2.8 convert_element_type.255
  889.7 15.4 %all-gather.19.cloned.1.call-done = bf16[512,1024]{1,0:T(8,128)(2,1)} async-done(((bf16[128,1024]{1,0:T(8,128)(2,1)}), bf16[512,1024]{1,0:T(8,128)(2,1)}) %all-gather.19.cloned.1.call-update) | async-done | bytes 1048592 | tf_op jit(solution)/shard_map/all_gather | solution.py:314
  905.1 2.8 convert_element_type.257
  (126 shorter events, 9.4 us)
Async XLA Ops:
  7.2 3.4 copy-start
  7.2 76.2 %all-gather.9.cloned.1.call-start = ((), (), s32[]{:S(2)}) async-start(), calls=%async_computation.4 | async-start | bytes 6488064 | tf_op jit(solution)/shard_map/all_gather | solution.py:299
  9.0 132.1 %all-gather.11.cloned.1.call-start = ((), (), s32[]{:S(2)}) async-start(), calls=%async_computation.5 | async-start | bytes 2162688 | tf_op jit(solution)/shard_map/all_gather | solution.py:299
  10.5 209.9 %all-gather.13.cloned.1.call-start = ((), (), s32[]{:S(2)}) async-start(), calls=%async_computation.6 | async-start | bytes 8650752 | tf_op jit(solution)/shard_map/all_gather | solution.py:299
  11.3 287.5 %all-gather.15.cloned.1.call-start = ((), (), s32[]{:S(2)}) async-start(), calls=%async_computation.7 | async-start | bytes 8650752 | tf_op jit(solution)/shard_map/all_gather | solution.py:299
  13.1 455.3 %reduce-scatter.9.cloned.1.call-start = ((), (), s32[]{:S(2)}) async-start(), calls=%async_computation.10 | async-start | bytes 8650752 | tf_op jit(solution)/shard_map/reduce_scatter | solution.py:313
  58.0 8.3 copy-start.3
  60.6 6.9 copy-start.27
  66.5 22.7 %copy-start.22 = (f32[512]{0:T(512)}, f32[512]{0:T(512)S(1)}, u32[]{:S(2)}) copy-start(f32[512]{0:T(512)S(1)} %broadcast_multiply_fusion.5) | copy-start | bytes 6148
  66.9 22.3 %copy-start.24 = (f32[512]{0:T(512)}, f32[512]{0:T(512)S(1)}, u32[]{:S(2)}) copy-start(f32[512]{0:T(512)S(1)} %add_rsqrt_fusion.1) | copy-start | bytes 6148
  67.5 21.7 %copy-start.20 = (f32[1024]{0:T(1024)}, f32[1024]{0:T(1024)S(1)}, u32[]{:S(2)}) copy-start(f32[1024]{0:T(1024)S(1)} %get-tuple-element.100) | copy-start | bytes 12292
  92.5 11.9 %copy-start.9 = (bf16[512,1024]{0,1:T(8,128)(2,1)}, bf16[512,1024]{0,1:T(8,128)(2,1)S(1)}, u32[]{:S(2)}) copy-start(bf16[512,1024]{0,1:T(8,128)(2,1)S(1)} %copy.65) | copy-start | bytes 3145732
  94.4 10.1 %copy-start.7 = (bf16[512,1024]{0,1:T(8,128)(2,1)}, bf16[512,1024]{0,1:T(8,128)(2,1)S(1)}, u32[]{:S(2)}) copy-start(bf16[512,1024]{0,1:T(8,128)(2,1)S(1)} %copy.66) | copy-start | bytes 3145732
  104.4 8.4 copy-start.13
  144.3 194.4 %copy-start.5 = (f32[512,1024]{1,0:T(8,128)}, f32[512,1024]{1,0:T(8,128)S(1)}, u32[]{:S(2)}) copy-start(f32[512,1024]{1,0:T(8,128)S(1)} %get-tuple-element.106) | copy-start | bytes 6291460
  220.4 78.4 %copy-start.15 = (bf16[512,1024]{1,0:T(8,128)(2,1)S(1)}, bf16[512,1024]{1,0:T(8,128)(2,1)}, u32[]{:S(2)}) copy-start(bf16[512,1024]{1,0:T(8,128)(2,1)} %param.18) | copy-start | bytes 3145732
  310.1 2.0 copy-start.30
  319.5 297.0 %reduce-scatter.11.cloned.1.call-start = ((), (), s32[]{:S(2)}) async-start(), calls=%async_computation.12 | async-start | bytes 8650752 | tf_op jit(solution)/shard_map/reduce_scatter | solution.py:313
  328.6 424.6 %reduce-scatter.7.cloned.1.call-start = ((), (), s32[]{:S(2)}) async-start(), calls=%async_computation.9 | async-start | bytes 2162688 | tf_op jit(solution)/shard_map/reduce_scatter | solution.py:313
  338.7 2.3 copy-start.14
  339.7 1.3 copy-start.12
  339.7 3.2 copy-start.18
  342.9 19.5 %copy-start.10 = (bf16[512,1024]{0,1:T(8,128)(2,1)}, bf16[512,1024]{0,1:T(8,128)(2,1)S(1)}, u32[]{:S(2)}) copy-start(bf16[512,1024]{0,1:T(8,128)(2,1)S(1)} %copy.68) | copy-start | bytes 3145732
  347.5 522.1 %reduce-scatter.5.cloned.1.call-start = ((), (), s32[]{:S(2)}) async-start(), calls=%async_computation.8 | async-start | bytes 6488064 | tf_op jit(solution)/shard_map/reduce_scatter | solution.py:313
  347.6 14.8 %slice-start = ((s8[16777216]{0:T(1024)(128)(4,1)}), s8[4194304]{0:T(1024)(128)(4,1)S(1)}, s32[]{:S(2)}) async-start(s8[16777216]{0:T(1024)(128)(4,1)} %bitcast.128), calls=%async_computation.14 | async-start | bytes 8388608
  347.6 14.8 %slice-start.1 = ((s8[16777216]{0:T(1024)(128)(4,1)}), s8[4194304]{0:T(1024)(128)(4,1)S(1)}, s32[]{:S(2)}) async-start(s8[16777216]{0:T(1024)(128)(4,1)} %bitcast.128), calls=%async_computation.15 | async-start | bytes 8388608
  347.6 15.8 %slice-start.2 = ((s8[16777216]{0:T(1024)(128)(4,1)}), s8[4194304]{0:T(1024)(128)(4,1)S(1)}, s32[]{:S(2)}) async-start(s8[16777216]{0:T(1024)(128)(4,1)} %bitcast.128), calls=%async_computation.16 | async-start | bytes 8388608
  347.6 17.0 %slice-start.3 = ((s8[16777216]{0:T(1024)(128)(4,1)}), s8[4194304]{0:T(1024)(128)(4,1)S(1)}, s32[]{:S(2)}) async-start(s8[16777216]{0:T(1024)(128)(4,1)} %bitcast.128), calls=%async_computation.17 | async-start | bytes 8388608
  375.2 6.6 copy-start.2
  375.2 6.6 copy-start.8
  381.8 1.5 copy-start.11
  381.8 1.5 copy-start.19
  383.3 9.9 %copy-start.16 = (bf16[512,1024]{1,0:T(8,128)(2,1)S(1)}, bf16[512,1024]{1,0:T(8,128)(2,1)}, u32[]{:S(2)}) copy-start(bf16[512,1024]{1,0:T(8,128)(2,1)} %fusion.30) | copy-start | bytes 3145732
  392.2 1.0 copy-start.17
  401.5 0.7 copy-start.26
  401.5 1.2 copy-start.4
  401.5 1.2 copy-start.21
  401.5 1.2 copy-start.23
  401.5 1.2 copy-start.25
  401.6 485.4 %all-gather.17.cloned.1.call-start = ((), (), s32[]{:S(2)}) async-start(), calls=%async_computation.11 | async-start | bytes 1310720 | tf_op jit(solution)/shard_map/all_gather | solution.py:314
  402.8 65.7 %copy-start.29 = (f32[1024]{0:T(1024)S(1)}, f32[1024]{0:T(1024)}, u32[]{:S(2)}) copy-start(f32[1024]{0:T(1024)} %get-tuple-element.61) | copy-start | bytes 12292
  411.3 205.3 %copy-start.6 = (f32[512,1024]{1,0:T(8,128)S(1)}, f32[512,1024]{1,0:T(8,128)}, u32[]{:S(2)}) copy-start(f32[512,1024]{1,0:T(8,128)} %copy-done.5) | copy-start | bytes 6291460
  411.3 205.3 %copy-start.28 = (f32[1024]{0:T(1024)S(1)}, f32[1024]{0:T(1024)}, u32[]{:S(2)}) copy-start(f32[1024]{0:T(1024)} %get-tuple-element.93) | copy-start | bytes 12292
  468.4 436.6 %all-gather.19.cloned.1.call-start = ((), (), s32[]{:S(2)}) async-start(), calls=%async_computation.13 | async-start | bytes 1310720 | tf_op jit(solution)/shard_map/all_gather | solution.py:314
  616.5 291.3 %copy-start.1 = (bf16[128,4096]{1,0:T(8,128)(2,1)S(1)}, bf16[128,4096]{1,0:T(8,128)(2,1)}, u32[]{:S(2)}) copy-start(bf16[128,4096]{1,0:T(8,128)(2,1)} %param.26) | copy-start | bytes 3145732
Sparse Core Ops, SparseCore 0:
  11.4 71.9 all-gather.8
  86.3 54.7 all-gather.10
  144.5 75.8 all-gather.12
  223.1 75.6 all-gather.14
  319.6 148.7 reduce-scatter.8
  470.6 145.8 reduce-scatter.10
  618.8 134.3 reduce-scatter.6
  758.8 110.8 reduce-scatter.4
  871.3 15.6 all-gather.16
  888.4 16.6 all-gather.18
